TPU v7x, 32 devices: a whole 2x2x4 slice. The times are simulated.
32 devices in a mesh: lon: 8 (over z, x), lat: 4 (over y, core).
Axes of the slice: x: 2, y: 2, z: 4, core: 2. Of those that a mesh axis runs over, the one named last changes fastest.
Arguments:
- grid_field: float32 [4, 64, 16, 2048], P(None, 'lat', None, 'lon'), may hold values from -6 to 6
- lat_weight: float32 [64], replicated, may hold values from 0.3 to 3
Outputs:
- spec_real: float32 [4, 64, 16, 1024], P(None, None, 'lat', 'lon')
- spec_imag: float32 [4, 64, 16, 1024], P(None, None, 'lat', 'lon')
All inputs are finite; a program needn't handle non-finite values.
Results may differ from a plain program's by a relative error of at most 0.000071.
Values sent between devices are 32-bit elements; how exact they have to be, the bound alone decides.
A program may use at most 64 MiB of HBM per device.

v0:
```python
import math

import jax
import jax.numpy as jnp
from jax import lax
from jax.sharding import PartitionSpec as P

MODES = 1024


two_pi = 2.0 * math.pi


def mode_table(lon_ids, mode_ids, length):
    phases = lon_ids[:, None] * mode_ids[None, :] % length
    angles = phases.astype(jnp.float32) * (two_pi / length)
    normalizer = 1.0 / math.sqrt(length)
    return (jnp.cos(angles) * normalizer, -jnp.sin(angles) * normalizer)


def per_device(grid_field, lat_weight):
    fields, lat_dev, radius_count, lon_dev = grid_field.shape
    cycle_size = lax.axis_size("lon")
    length = cycle_size * lon_dev
    mode_dev = MODES // cycle_size
    my_index = lax.axis_index("lon")
    row_count = fields * lat_dev * radius_count
    flat_grid = grid_field.reshape(row_count, lon_dev)
    mode_ids = my_index * mode_dev + jnp.arange(mode_dev, dtype=jnp.int32)
    lon_block = lax.all_gather(flat_grid, "lon", axis=1, tiled=True)
    lon_ids = jnp.arange(lon_block.shape[1], dtype=jnp.int32)
    cosine, sine_part = mode_table(lon_ids, mode_ids, length)
    dft_table = jnp.concatenate([cosine, sine_part], axis=1)
    summed = jnp.dot(
        lon_block, dft_table, precision=lax.Precision.HIGHEST, preferred_element_type=jnp.float32
    )
    spectra = summed.reshape(fields, lat_dev, radius_count, 2, mode_dev)
    gathered = lax.all_to_all(spectra, "lat", split_axis=2, concat_axis=1, tiled=True)
    weights_row = lat_weight[None, :, None, None]
    return (gathered[:, :, :, 0, :] * weights_row, gathered[:, :, :, 1, :] * weights_row)


def solution(mesh):
    in_specs = (P(None, "lat", None, "lon"), P())
    out_specs = (P(None, None, "lat", "lon"), P(None, None, "lat", "lon"))
    return jax.shard_map(
        per_device, mesh=mesh, in_specs=in_specs, out_specs=out_specs, check_vma=False
    )
```

profile of v0, /device:TPU:0, one launch (start us, length us, event | category | flops | bytes accessed | tf_op | source)
XLA Modules:
  0.0 181.7 jit_solution(17533059803057809148)
XLA Ops:
  7.2 0.0 all-gather.2.cloned.1.call-start
  7.2 0.7 all-gather.2.cloned.1.call-update
  7.9 4.2 %cosine_multiply_fusion = (f32[2048,128]{1,0:T(8,128)S(1)}, f32[2048,128]{1,0:T(8,128)S(1)}) fusion(s32[128]{0:T(128)S(1)} %iota_add_fusion), kind=kLoop, calls=%fused_computation.12 | loop fusion | flops 4456448 | bytes 2097664 | tf_op jit(solution)/shard_map/mul | solution.py:18
  12.1 125.6 %all-gather.2.cloned.1.call-done = f32[1024,2048]{1,0:T(8,128)} async-done(((f32[1024,256]{1,0:T(8,128)}), f32[1024,2048]{1,0:T(8,128)}) %all-gather.2.cloned.1.call-update) | async-done | bytes 8388624 | tf_op jit(solution)/shard_map/all_gather | solution.py:30
  137.7 15.9 %fusion.4 = f32[1024,256]{0,1:T(8,128)S(1)} fusion(f32[1024,2048]{1,0:T(8,128)} %all-gather.2.cloned.1.call-done, f32[2048,128]{1,0:T(8,128)S(1)} %get-tuple-element.9, f32[2048,128]{1,0:T(8,128)S(1)} %get-tuple-element.8), kind=kOutput, calls=%fused_computation.7 | convolution fusion | flops 6442975232 | bytes 11534336 | tf_op jit(solution)/shard_map/dot_general | solution.py:34
  153.6 0.0 copy-start
  153.6 0.3 copy.13
  154.0 0.5 reshape.16
  154.5 0.6 copy.14
  155.1 17.0 %all_to_all.18 = f32[4,16,16,2,128]{4,3,1,0,2:T(2,128)S(1)} all-to-all(f32[4,16,16,2,128]{4,3,1,0,2:T(2,128)S(1)} %copy.14), channel_id=1, replica_groups=mesh['lon'=8,'lat'=4] {'lat'}, dimensions={2} | all-to-all | bytes 2097152 | tf_op jit(solution)/shard_map/all_to_all | solution.py:38
  172.1 0.1 copy.15
  172.2 0.1 copy.16
  172.4 0.0 copy-done
  172.4 0.2 fusion.13
  172.6 1.1 copy.19
  173.7 1.1 copy.18
  (1 shorter events, 0.0 us)
Async XLA Ops:
  7.2 130.5 %all-gather.2.cloned.1.call-start = ((), (), s32[]{:S(2)}) async-start(), calls=%async_computation.1 | async-start | bytes 9437184 | tf_op jit(solution)/shard_map/all_gather | solution.py:30
  153.6 18.8 %copy-start = (f32[64]{0:T(128)S(1)}, f32[64]{0:T(128)}, u32[]{:S(2)}) copy-start(f32[64]{0:T(128)} %param.3) | copy-start | bytes 772
Sparse Core Ops, SparseCore 0:
  10.0 127.6 all-gather.1
where the time goes:
time: 182 us
  waiting for transfers between devices  126 us (69%)
  blocking collectives  17 us (9%)
  matrix products  15.9 us (9%)
  between operations  14.1 us (8%)
  other arithmetic  4.36 us (2%)
  local copies, waits for them, and re-layouts  3.95 us (2%)
    all_gather x1, waiting for transfers between devices, per_device(): lon_block = lax.all_gather(flat_grid, 'lon', axis=1, tiled=True)  126 us
    all_to_all x1, blocking collectives, per_device(): lax.all_to_all(spectra, 'lat', split_axis=2, concat_axis=1, tiled=True)  17 us
    dot_general x1, matrix products, per_device(): jnp.dot(lon_block, dft_table, precision=lax.Precision.HIGHEST, preferred_...  15.9 us
    mul x1, other arithmetic, mode_table(): return (jnp.cos(angles) * normalizer, -jnp.sin(angles) * normalizer)  4.17 us
  transfers between devices with their start and end apart: 1, of which 1 were waited for; matrix products, arithmetic and copies ran while one was open for 2% of the time, Pallas kernels for 0%

commit v1 on v0

v1 whole, which is shorter than its diff:
```python
import functools
import math

import jax
import jax.numpy as jnp
import numpy as np
from jax import lax
from jax.experimental import pallas as pl
from jax.experimental.pallas import tpu as pltpu
from jax.sharding import PartitionSpec as P

MODES = 1024
CHUNKS = 4
LANES = 128
MESH = pl.DeviceIdType.MESH


def tables(cycle, lon_dev, width):
    length = cycle * lon_dev
    j = np.arange(lon_dev, dtype=np.int64)
    phase = np.arange(cycle)[:, None] * j[None, :] % length * (2.0 * math.pi / length)
    twiddle = np.stack([np.cos(phase), -np.sin(phase)]).astype(np.float32)
    phase = j[:, None] * np.arange(width)[None, :] % lon_dev * (2.0 * math.pi / lon_dev)
    real, imag = np.cos(phase) / math.sqrt(length), -np.sin(phase) / math.sqrt(length)
    dft = np.block([[real, imag], [-imag, real]]).astype(np.float32)
    high = dft.astype(jnp.bfloat16)
    low = (dft - high.astype(np.float32)).astype(jnp.bfloat16)
    return twiddle, np.stack([high, low])


def kernel(
    cycle, groups, chunks, part, lat_dev, mode_dev,
    x_ref, weight_ref, twiddle_hbm, dft_hbm, out_ref,
    held, stage, twiddle, dft, b_high, b_low,
    table_sem, send_sem, held_sem, stage_sem, out_sem,
):
    lon, lat = lax.axis_index("lon"), lax.axis_index("lat")
    me = lon * groups + lat
    everyone = cycle * groups
    rows_dev = chunks * part
    radii, lon_dev = x_ref.shape[1], x_ref.shape[2]
    radii_dev = radii // groups
    rows = part * radii
    width = dft.shape[2] // 2

    table_copies = [
        pltpu.make_async_copy(twiddle_hbm, twiddle, table_sem.at[0]),
        pltpu.make_async_copy(dft_hbm, dft, table_sem.at[1]),
    ]
    for copy in table_copies:
        copy.start()

    def own(c):
        return pltpu.make_async_copy(
            x_ref.at[pl.ds(lon * rows_dev + c * part, part)], held.at[c, lon], held_sem.at[c]
        )

    for c in range(chunks):
        own(c).start()

    barrier = pltpu.get_barrier_semaphore()

    @pl.loop(1, everyone)
    def _(i):
        peer = lax.rem(me + i, everyone)
        pl.semaphore_signal(
            barrier, inc=1, device_id={"lon": peer // groups, "lat": lax.rem(peer, groups)},
            device_id_type=MESH,
        )

    pl.semaphore_wait(barrier, everyone - 1)

    for c in range(chunks):
        for i in range(1, cycle):
            peer = lax.rem(lon + i, cycle)
            pltpu.make_async_remote_copy(
                src_ref=x_ref.at[pl.ds(peer * rows_dev + c * part, part)],
                dst_ref=held.at[c, lon],
                send_sem=send_sem,
                recv_sem=held_sem.at[c],
                device_id={"lon": peer},
                device_id_type=MESH,
            ).start()

    for copy in table_copies:
        copy.wait()

    lane = lax.broadcasted_iota(jnp.int32, (rows, width), 1)
    residue = lax.rem(lane, cycle)
    step = lane // cycle

    def chunk(c, carry):
        pltpu.make_async_copy(held.at[c], held.at[c], held_sem.at[c]).wait()
        blocks = [held[c, l].reshape(rows, lon_dev) for l in range(cycle)]
        for s in range(cycle // 2 + 1):
            real = imag = None
            for l in range(cycle):
                angle = 2.0 * math.pi * (l * s % cycle) / cycle
                co, si = math.cos(angle), -math.sin(angle)
                if abs(co) > 1e-9:
                    term = blocks[l] * np.float32(co)
                    real = term if real is None else real + term
                if abs(si) > 1e-9:
                    term = blocks[l] * np.float32(si)
                    imag = term if imag is None else imag + term
            for t in sorted({s, (cycle - s) % cycle}):
                sign = 1.0 if t == s else -1.0
                tr, ti = twiddle[0, t:t + 1, :], twiddle[1, t:t + 1, :]
                if imag is None:
                    re, im = real * tr, real * ti
                else:
                    re = real * tr - imag * (ti * sign)
                    im = real * ti + imag * (tr * sign)
                for part_of, at in ((re, 0), (im, lon_dev)):
                    high = part_of.astype(jnp.bfloat16)
                    b_high[t * rows:(t + 1) * rows, at:at + lon_dev] = high
                    b_low[t * rows:(t + 1) * rows, at:at + lon_dev] = (
                        part_of - high.astype(jnp.float32)
                    ).astype(jnp.bfloat16)
        dot = functools.partial(jnp.dot, preferred_element_type=jnp.float32)
        z = dot(b_high[...], dft[0]) + dot(b_low[...], dft[0]) + dot(b_high[...], dft[1])
        first = lon * rows_dev + c * part
        time = lat * lat_dev + lax.rem(first, lat_dev)
        scale = [weight_ref[time + p] for p in range(part)]
        for owner in range(cycle):
            index = step + owner * (mode_dev // cycle)
            index = jnp.minimum(index, width - 1)
            for half in range(2):
                value = None
                for s in range(cycle):
                    piece = jnp.take_along_axis(
                        z[s * rows:(s + 1) * rows, half * width:(half + 1) * width],
                        index, axis=1, mode="promise_in_bounds",
                    )
                    value = piece if value is None else jnp.where(residue == s, piece, value)
                for p in range(part):
                    scaled = value[p * radii:(p + 1) * radii] * scale[p]
                    for g in range(groups):
                        stage[c, owner * groups + g, half, p] = scaled[
                            g * radii_dev:(g + 1) * radii_dev, :mode_dev
                        ]
        field = first // lat_dev
        target = out_ref.at[:, field, pl.ds(time, part)]
        pltpu.make_async_copy(stage.at[c, me], target, out_sem).start()

        @pl.loop(1, everyone)
        def _(i):
            peer = lax.rem(me + i, everyone)
            pltpu.make_async_remote_copy(
                src_ref=stage.at[c, peer],
                dst_ref=target,
                send_sem=stage_sem,
                recv_sem=out_sem,
                device_id={"lon": peer // groups, "lat": lax.rem(peer, groups)},
                device_id_type=MESH,
            ).start()

        return carry

    lax.fori_loop(0, chunks, chunk, 0)

    sent = x_ref.at[pl.ds(0, (cycle - 1) * rows_dev)]
    pltpu.make_async_copy(sent, sent, send_sem).wait()
    for c in range(chunks):
        staged = stage.at[c, pl.ds(0, everyone - 1)]
        pltpu.make_async_copy(staged, staged, stage_sem).wait()
    pltpu.make_async_copy(out_ref, out_ref, out_sem).wait()


def per_device(grid_field, lat_weight):
    fields, lat_dev, radii, lon_dev = grid_field.shape
    cycle, groups = lax.axis_size("lon"), lax.axis_size("lat")
    mode_dev = MODES // cycle
    width = -(-mode_dev // LANES) * LANES
    rows_dev = fields * lat_dev // cycle
    part = max(1, rows_dev // CHUNKS)
    chunks = rows_dev // part
    rows = part * radii
    twiddle, dft = tables(cycle, lon_dev, width)
    out = pl.pallas_call(
        functools.partial(kernel, cycle, groups, chunks, part, lat_dev, mode_dev),
        out_shape=jax.ShapeDtypeStruct(
            (2, fields, lat_dev * groups, radii // groups, mode_dev), jnp.float32
        ),
        in_specs=[
            pl.BlockSpec(memory_space=pl.ANY),
            pl.BlockSpec(memory_space=pltpu.SMEM),
            pl.BlockSpec(memory_space=pl.ANY),
            pl.BlockSpec(memory_space=pl.ANY),
        ],
        out_specs=pl.BlockSpec(memory_space=pltpu.VMEM),
        scratch_shapes=[
            pltpu.VMEM((chunks, cycle, part, radii, lon_dev), jnp.float32),
            pltpu.VMEM((chunks, cycle * groups, 2, part, radii // groups, mode_dev), jnp.float32),
            pltpu.VMEM(twiddle.shape, jnp.float32),
            pltpu.VMEM(dft.shape, jnp.bfloat16),
            pltpu.VMEM((cycle * rows, 2 * lon_dev), jnp.bfloat16),
            pltpu.VMEM((cycle * rows, 2 * lon_dev), jnp.bfloat16),
            pltpu.SemaphoreType.DMA((2,)),
            pltpu.SemaphoreType.DMA,
            pltpu.SemaphoreType.DMA((chunks,)),
            pltpu.SemaphoreType.DMA,
            pltpu.SemaphoreType.DMA,
        ],
        compiler_params=pltpu.CompilerParams(collective_id=0, has_side_effects=True),
    )(
        grid_field.reshape(fields * lat_dev, radii, lon_dev), lat_weight,
        jnp.asarray(twiddle), jnp.asarray(dft),
    )
    return out[0], out[1]


def solution(mesh):
    in_specs = (P(None, "lat", None, "lon"), P())
    out_specs = (P(None, None, "lat", "lon"), P(None, None, "lat", "lon"))
    return jax.shard_map(
        per_device, mesh=mesh, in_specs=in_specs, out_specs=out_specs, check_vma=False
    )
```

time: 182 us -> 56.6 us (0.31)
  waiting for transfers between devices: 126 us -> 0 us
  Pallas kernels: 0 us -> 53.6 us
  blocking collectives: 17 us -> 0 us
  matrix products: 15.9 us -> 0 us
  between operations: 14.1 us -> 0.64 us
  other arithmetic: 4.36 us -> 0 us
    all_gather x1 -> x0, waiting for transfers between devices: 126 us -> none  [per_device(): lon_block = lax.all_gather(flat_grid, 'lon', axis=1, tiled=True)]
    pallas_call x0 -> x1, Pallas kernels: none -> 53.6 us  [per_device(): pl.pallas_call(functools.partial(kernel, cycle, groups, chunks, part, lat...]
    all_to_all x1 -> x0, blocking collectives: 17 us -> none  [per_device(): lax.all_to_all(spectra, 'lat', split_axis=2, concat_axis=1, tiled=True)]
    dot_general x1 -> x0, matrix products: 15.9 us -> none  [per_device(): jnp.dot(lon_block, dft_table, precision=lax.Precision.HIGHEST, preferred_...]
    mul x2 -> x0, other arithmetic: 4.35 us -> none  [the longest x1 4.17 us: mode_table(): return (jnp.cos(angles) * normalizer, -jnp.sin(angles) * normalizer)]
    unnamed x4 -> x0, local copies, waits for them, and re-layouts: 2.28 us -> none
    squeeze x0 -> x1, local copies, waits for them, and re-layouts: none -> 2.24 us  [per_device(): return (out[0], out[1])]
  transfers between devices with their start and end apart: 1 -> 0, of which waited for: 1 -> 0; matrix products, arithmetic and copies ran while one was open for 2% -> 0% of each run, Pallas kernels for 0% -> 0%
where the time goes in v1:
time: 56.6 us; the launch traced here: 56.5 us
  Pallas kernels  53.6 us (95%)
  local copies, waits for them, and re-layouts  2.24 us (4%)
  between operations  0.64 us (1%)
    pallas_call x1, Pallas kernels, per_device(): pl.pallas_call(functools.partial(kernel, cycle, groups, chunks, part, lat...  53.6 us
    squeeze x1, local copies, waits for them, and re-layouts, per_device(): return (out[0], out[1])  2.24 us

profile of v1, /device:TPU:0, one launch (start us, length us, event | category | flops | bytes accessed | tf_op | source)
XLA Modules:
  0.0 56.5 jit_solution(14067973961773559624)
XLA Ops:
  0.6 53.6 %shard_map.59 = f32[2,4,64,4,128]{4,3,2,1,0:T(4,128)} custom-call(f32[64,16,256]{2,1,0:T(8,128)} %bitcast.5, f32[64]{0:T(128)} %weight_ref.1, f32[2,8,256]{2,1,0:T(8,128)} %constant.4.clone.twiddle_hbm, bf16[2,512,256]{2,1,0:T(8,128)(2,1)} %constant.5.clone.dft_hbm), custom_call_target="tpu_custom_call" | custom-call | tf_op jit(solution)/shard_map/pallas_call | solution.py:180
  54.2 2.2 %slice_bitcast_fusion = (f32[4,64,4,128]{3,2,1,0:T(4,128)}, f32[4,64,4,128]{3,2,1,0:T(4,128)}) fusion(f32[2,4,64,4,128]{4,3,2,1,0:T(4,128)} %shard_map.59), kind=kLoop, calls=%fused_computation | loop fusion | bytes 2097152 | tf_op jit(solution)/shard_map/squeeze | solution.py:210

commit v2 on v1

--- a/solution.py
+++ b/solution.py
@@ -30,9 +30,9 @@
 
 def kernel(
     cycle, groups, chunks, part, lat_dev, mode_dev,
-    x_ref, weight_ref, twiddle_hbm, dft_hbm, out_ref,
+    x_ref, weight_hbm, twiddle_hbm, dft_hbm, out_ref,
     held, stage, twiddle, dft, b_high, b_low,
-    table_sem, send_sem, held_sem, stage_sem, out_sem,
+    weight_ref, flood_sem, table_sem, send_sem, held_sem, stage_sem, out_sem,
 ):
     lon, lat = lax.axis_index("lon"), lax.axis_index("lat")
     me = lon * groups + lat
@@ -46,6 +46,7 @@
     table_copies = [
         pltpu.make_async_copy(twiddle_hbm, twiddle, table_sem.at[0]),
         pltpu.make_async_copy(dft_hbm, dft, table_sem.at[1]),
+        pltpu.make_async_copy(weight_hbm, weight_ref, table_sem.at[2]),
     ]
     for copy in table_copies:
         copy.start()
@@ -58,29 +59,52 @@
     for c in range(chunks):
         own(c).start()
 
-    barrier = pltpu.get_barrier_semaphore()
-
-    @pl.loop(1, everyone)
-    def _(i):
-        peer = lax.rem(me + i, everyone)
-        pl.semaphore_signal(
-            barrier, inc=1, device_id={"lon": peer // groups, "lat": lax.rem(peer, groups)},
+    def send(c, peer):
+        pltpu.make_async_remote_copy(
+            src_ref=x_ref.at[pl.ds(peer * rows_dev + c * part, part)],
+            dst_ref=held.at[c, lon],
+            send_sem=send_sem,
+            recv_sem=held_sem.at[c],
+            device_id={"lon": peer},
             device_id_type=MESH,
-        )
-
-    pl.semaphore_wait(barrier, everyone - 1)
-
-    for c in range(chunks):
+        ).start()
+
+    lon_row, lon_side = lon // 2, lax.rem(lon, 2)
+    lat_row, lat_side = lat // 2, lax.rem(lat, 2)
+    neighbours = [
+        (lon_row > 0, lon - 2, lat),
+        (lon_row < cycle // 2 - 1, lon + 2, lat),
+        (lon_side >= 0, lon + 1 - 2 * lon_side, lat),
+        (lat_row > 0, lon, lat - 2),
+        (lat_row < groups // 2 - 1, lon, lat + 2),
+        (lat_side >= 0, lon, lat + 1 - 2 * lat_side),
+    ]
+
+    def flood(sem):
+        for present, to_lon, to_lat in neighbours:
+            @pl.when(present)
+            def _():
+                pl.semaphore_signal(
+                    sem, inc=1, device_id={"lon": to_lon, "lat": to_lat}, device_id_type=MESH
+                )
+        pl.semaphore_wait(sem, sum(jnp.where(present, 1, 0) for present, _, _ in neighbours))
+
+    for r in range(1, cycle // 2 + 1):
+        flood(pltpu.get_barrier_semaphore() if r == 1 else flood_sem.at[r - 2])
+        for step, side in ((r, lon_side), (r - 1, 1 - lon_side)):
+            for way in ((1, -1) if step else (1,)):
+                row = lon_row + way * step
+
+                @pl.when((row >= 0) & (row < cycle // 2))
+                def _():
+                    send(0, 2 * row + side)
+
+    for c in range(1, chunks):
         for i in range(1, cycle):
-            peer = lax.rem(lon + i, cycle)
-            pltpu.make_async_remote_copy(
-                src_ref=x_ref.at[pl.ds(peer * rows_dev + c * part, part)],
-                dst_ref=held.at[c, lon],
-                send_sem=send_sem,
-                recv_sem=held_sem.at[c],
-                device_id={"lon": peer},
-                device_id_type=MESH,
-            ).start()
+            send(c, lax.rem(lon + i, cycle))
+
+    for r in range(cycle // 2 + 1, cycle // 2 + groups // 2 + 1):
+        flood(flood_sem.at[r - 2])
 
     for copy in table_copies:
         copy.wait()
@@ -167,6 +191,17 @@
     pltpu.make_async_copy(out_ref, out_ref, out_sem).wait()
 
 
+def split(both_ref, real_ref, imag_ref, sem):
+    copies = [
+        pltpu.make_async_copy(both_ref.at[i, f], ref.at[f], sem.at[i, f])
+        for i, ref in enumerate((real_ref, imag_ref)) for f in range(ref.shape[0])
+    ]
+    for copy in copies:
+        copy.start()
+    for copy in copies:
+        copy.wait()
+
+
 def per_device(grid_field, lat_weight):
     fields, lat_dev, radii, lon_dev = grid_field.shape
     cycle, groups = lax.axis_size("lon"), lax.axis_size("lat")
@@ -179,12 +214,12 @@
     twiddle, dft = tables(cycle, lon_dev, width)
     out = pl.pallas_call(
         functools.partial(kernel, cycle, groups, chunks, part, lat_dev, mode_dev),
-        out_shape=jax.ShapeDtypeStruct(
+        out_shape=pltpu.VMEM(
             (2, fields, lat_dev * groups, radii // groups, mode_dev), jnp.float32
         ),
         in_specs=[
             pl.BlockSpec(memory_space=pl.ANY),
-            pl.BlockSpec(memory_space=pltpu.SMEM),
+            pl.BlockSpec(memory_space=pl.ANY),
             pl.BlockSpec(memory_space=pl.ANY),
             pl.BlockSpec(memory_space=pl.ANY),
         ],
@@ -196,18 +231,28 @@
             pltpu.VMEM(dft.shape, jnp.bfloat16),
             pltpu.VMEM((cycle * rows, 2 * lon_dev), jnp.bfloat16),
             pltpu.VMEM((cycle * rows, 2 * lon_dev), jnp.bfloat16),
-            pltpu.SemaphoreType.DMA((2,)),
+            pltpu.SMEM(lat_weight.shape, jnp.float32),
+            pltpu.SemaphoreType.REGULAR((cycle // 2 + groups // 2 - 1,)),
+            pltpu.SemaphoreType.DMA((3,)),
             pltpu.SemaphoreType.DMA,
             pltpu.SemaphoreType.DMA((chunks,)),
             pltpu.SemaphoreType.DMA,
             pltpu.SemaphoreType.DMA,
         ],
-        compiler_params=pltpu.CompilerParams(collective_id=0, has_side_effects=True),
+        compiler_params=pltpu.CompilerParams(collective_id=0, has_side_effects=True, vmem_limit_bytes=67_043_328 - 5 * 2**18),
     )(
         grid_field.reshape(fields * lat_dev, radii, lon_dev), lat_weight,
         jnp.asarray(twiddle), jnp.asarray(dft),
     )
-    return out[0], out[1]
+    half = jax.ShapeDtypeStruct(out.shape[1:], jnp.float32)
+    return pl.pallas_call(
+        split,
+        out_shape=(half, half),
+        in_specs=[pl.BlockSpec(memory_space=pltpu.VMEM)],
+        out_specs=(pl.BlockSpec(memory_space=pl.ANY), pl.BlockSpec(memory_space=pl.ANY)),
+        scratch_shapes=[pltpu.SemaphoreType.DMA((2, fields))],
+        compiler_params=pltpu.CompilerParams(vmem_limit_bytes=16 * 2**20),
+    )(out)
 
 
 def solution(mesh):

time: 56.6 us -> 53.6 us (0.947)
  local copies, waits for them, and re-layouts: 2.24 us -> 0 us
  Pallas kernels: 53.6 us -> 52.8 us
    squeeze x1 -> x0, local copies, waits for them, and re-layouts: 2.24 us -> none  [per_device(): return (out[0], out[1])]
    pallas_call x1, Pallas kernels: 53.6 us -> 51.8 us  [per_device(): pl.pallas_call(functools.partial(kernel, cycle, groups, chunks, part, lat...]
    pallas_call x0 -> x1, Pallas kernels: none -> 1.03 us  [per_device(): pl.pallas_call(split, out_shape=(half, half), in_specs=[pl.BlockSpec(memo...]
where the time goes in v2:
time: 53.6 us; the launch traced here: 53.5 us
  Pallas kernels  52.8 us (99%)
  between operations  0.64 us (1%)
    pallas_call x1, Pallas kernels, per_device(): pl.pallas_call(functools.partial(kernel, cycle, groups, chunks, part, lat...  51.8 us

profile of v2, /device:TPU:0, one launch (start us, length us, event | category | flops | bytes accessed | tf_op | source)
XLA Modules:
  0.0 53.5 jit_solution(2248417250273581000)
XLA Ops:
  0.6 51.8 %shard_map.59.both_ref = f32[2,4,64,4,128]{4,3,2,1,0:T(4,128)S(1)} custom-call(f32[64,16,256]{2,1,0:T(8,128)} %bitcast.1, f32[64]{0:T(128)} %weight_hbm.1, f32[2,8,256]{2,1,0:T(8,128)} %constant.4.clone.twiddle_hbm, bf16[2,512,256]{2,1,0:T(8,128)(2,1)} %constant.5.clone.dft_hbm), custom_call_target="tpu_custom_call" | custom-call | tf_op jit(solution)/shard_map/pallas_call | solution.py:215
  52.5 1.0 %shard_map.60 = (f32[4,64,4,128]{3,2,1,0:T(4,128)}, f32[4,64,4,128]{3,2,1,0:T(4,128)}) custom-call(f32[2,4,64,4,128]{4,3,2,1,0:T(4,128)S(1)} %shard_map.59.both_ref), custom_call_target="tpu_custom_call" | custom-call | tf_op jit(solution)/shard_map/pallas_call | solution.py:248

commit v3 on v2

--- a/solution.py
+++ b/solution.py
@@ -10,7 +10,7 @@
 from jax.sharding import PartitionSpec as P
 
 MODES = 1024
-CHUNKS = 4
+CHUNKS = 2
 LANES = 128
 MESH = pl.DeviceIdType.MESH
 

time: 53.6 us -> 52 us (0.970); the launches traced: 53.5 us -> 50.9 us
  Pallas kernels: 52.8 us -> 50.3 us
    pallas_call x1, Pallas kernels: 51.8 us -> 49.3 us  [per_device(): pl.pallas_call(functools.partial(kernel, cycle, groups, chunks, part, lat...]
where the time goes in v3:
time: 52 us; the launch traced here: 50.9 us
  Pallas kernels  50.3 us (97%)
  between operations  0.64 us (1%)
    pallas_call x1, Pallas kernels, per_device(): pl.pallas_call(functools.partial(kernel, cycle, groups, chunks, part, lat...  49.3 us

profile of v3, /device:TPU:0, one launch (start us, length us, event | category | flops | bytes accessed | tf_op | source)
XLA Modules:
  0.0 50.9 jit_solution(15712596149503664698)
XLA Ops:
  0.6 49.3 %shard_map.59.both_ref = f32[2,4,64,4,128]{4,3,2,1,0:T(4,128)S(1)} custom-call(f32[64,16,256]{2,1,0:T(8,128)} %bitcast.1, f32[64]{0:T(128)} %weight_hbm.1, f32[2,8,256]{2,1,0:T(8,128)} %constant.4.clone.twiddle_hbm, bf16[2,512,256]{2,1,0:T(8,128)(2,1)} %constant.5.clone.dft_hbm), custom_call_target="tpu_custom_call" | custom-call | tf_op jit(solution)/shard_map/pallas_call | solution.py:215
  49.9 1.0 %shard_map.60 = (f32[4,64,4,128]{3,2,1,0:T(4,128)}, f32[4,64,4,128]{3,2,1,0:T(4,128)}) custom-call(f32[2,4,64,4,128]{4,3,2,1,0:T(4,128)S(1)} %shard_map.59.both_ref), custom_call_target="tpu_custom_call" | custom-call | tf_op jit(solution)/shard_map/pallas_call | solution.py:248
